TPU v7x, 512 devices: a whole 4x4x16 slice. The times are simulated.
512 devices in a mesh: rows: 32 (over x, y, core), upd: 16 (over z).
Axes of the slice: x: 4, y: 4, z: 16, core: 2. Of those that a mesh axis runs over, the one named last changes fastest.
Arguments:
- tile_factors: bfloat16 [32, 128, 1024, 128], P('rows', 'upd'), may hold values from -6 to 6
- panel_factors: bfloat16 [128, 1024, 128], P('upd', 'rows'), may hold values from -0.1875 to 0.1875
- nonnull: int32 [32, 128], P('rows', 'upd'), may hold values from 0 to 1, as said below
- sketch: float32 [64, 1024], replicated, may hold values from -6 to 6
Outputs:
- update_factors: float32 [32, 1024, 128], P('rows', 'upd')
Inputs may be any that keep to these rules, and one draw needn't show every extreme that they name: In every aligned block of 8 update indices the first one is nonnull for every tile row.
All inputs are finite; a program needn't handle non-finite values.
Results may differ from a plain program's by a relative error of at most 0.0003.
Values may be sent and summed in bfloat16 or wider, within the bound.
No kernel may reach another device: no remote copies, remote signals or barrier semaphores. Data moves between devices by JAX's collectives and lax.ppermute only.
A program may use at most 64 MiB of HBM per device.

v0:
```python
import jax
import jax.numpy as jnp
from jax import lax
from jax.sharding import PartitionSpec as P


def from_partner(shard, axis, stride):
    return lax.ppermute(shard, axis, [(i, i ^ 1 << stride) for i in range(lax.axis_size(axis))])


def compress(lefts, rights, sketch):
    hi = lax.Precision.HIGHEST
    proj = jnp.einsum("nbr,sb->nrs", rights, sketch, precision=hi)
    span = jnp.einsum("nbr,nrs->bs", lefts, proj, precision=hi)
    gram = jnp.dot(span.T, span, precision=hi)
    order = gram.shape[0]
    shift = 0.001 * jnp.trace(gram) / order + 1e-20
    gram = gram + shift * jnp.eye(order, dtype=gram.dtype)
    chol = jnp.linalg.cholesky(gram)
    basis = lax.linalg.triangular_solve(chol, span, left_side=False, lower=True, transpose_a=True)
    coef = jnp.einsum("nbr,bs->nrs", lefts, basis, precision=hi)
    image = jnp.einsum("nbr,nrs->bs", rights, coef, precision=hi)
    return (basis, image)


def merge_pair(pair, sketch, rank):
    basis, image = compress(pair[:, :, :rank], pair[:, :, rank:], sketch)
    return jnp.concatenate([basis, image], axis=-1)


def body(tile_factors, panel_factors, nonnull, sketch):
    rank = tile_factors.shape[3] // 2
    tiles = tile_factors[0]
    own_right = tiles[:, :, rank:]
    panel = lax.all_gather(panel_factors, "rows", axis=1, tiled=True)
    inner = jnp.einsum(
        "kbr,kbs->krs", own_right, panel[:, :, rank:], preferred_element_type=jnp.float32
    )
    far_left = panel[:, :, :rank]
    weight = nonnull[0].astype(jnp.float32)
    lefts = jnp.einsum(
        "kbr,krs->kbs",
        tiles[:, :, :rank].astype(jnp.float32),
        inner,
        precision=lax.Precision.HIGHEST,
    )
    lefts = lefts * weight[:, None, None]
    basis, image = compress(lefts, far_left.astype(jnp.float32), sketch)
    packed = jnp.concatenate([basis, image], axis=-1)
    levels = lax.axis_size("upd").bit_length() - 1
    for level in range(levels):
        other = from_partner(packed, "upd", level)
        upper = lax.axis_index("upd") >> level & 1 == 1
        low = jnp.where(upper, other, packed)
        high = jnp.where(upper, packed, other)
        packed = merge_pair(jnp.stack([low, high]), sketch, rank)
    scale = jnp.float32(packed.shape[0]) ** 0.5
    result = jnp.concatenate([packed[:, :rank] * scale, packed[:, rank:] / scale], axis=-1)
    share = packed.shape[0] // lax.axis_size("upd")
    mine = lax.dynamic_slice_in_dim(result, lax.axis_index("upd") * share, share, 0)
    return mine[None]


def solution(mesh):
    in_specs = (P("rows", "upd", None, None), P("upd", "rows", None), P("rows", "upd"), P())
    out_specs = P("rows", "upd", None)
    return jax.shard_map(body, mesh=mesh, in_specs=in_specs, out_specs=out_specs, check_vma=False)
```

profile of v0, /device:TPU:1, one launch (start us, length us, event | category | flops | bytes accessed | tf_op | source)
XLA Modules:
  0.0 328.8 jit_solution(11202653416886925605)
XLA Ops:
  6.5 1.5 copy.41
  8.1 2.9 copy.40
  11.0 64.0 %all-gather.2.cloned.1.call-done = bf16[8,1024,128]{2,0,1:T(8,128)(2,1)} async-done(((bf16[8,32,128]{2,0,1:T(8,128)(2,1)}), bf16[8,1024,128]{2,0,1:T(8,128)(2,1)}) %all-gather.2.cloned.1.call-update) | async-done | bytes 2097168 | tf_op jit(solution)/shard_map/all_gather | solution.py:35
  75.1 4.3 %fusion.93 = (bf16[8,1024,64]{2,0,1:T(8,128)(2,1)}, bf16[8,1024,64]{2,0,1:T(8,128)(2,1)S(1)}) fusion(bf16[8,1024,128]{2,0,1:T(8,128)(2,1)} %all-gather.2.cloned.1.call-done), kind=kLoop, calls=%fused_computation.149 | loop fusion | bytes 4194304 | tf_op jit(solution)/shard_map/slice | solution.py:39
  79.4 0.8 fusion
  80.1 2.2 fusion.12
  82.3 2.5 copy.88
  84.9 1.6 fusion.38
  86.5 1.6 fusion.8
  88.1 0.7 copy-done.2
  88.8 1.0 select_reduce_fusion.5
  90.5 5.8 %cholesky.89 = f32[64,64]{1,0:T(8,128)S(1)} custom-call(f32[64,64]{1,0:T(8,128)S(1)} %fusion.68), custom_call_target="Cholesky" | custom-call | tf_op jit(solution)/shard_map/jit(cholesky)/cholesky | solution.py:19
  97.1 0.7 fusion.49
  97.7 4.9 %custom-call.9 = f32[1,64,64]{1,2,0:T(8,128)S(1)} custom-call(f32[1,64,64]{2,1,0:T(8,128)S(1)} %fusion.49), custom_call_target="InvertDiagBlocksLowerTriangular" | custom-call | tf_op jit(solution)/shard_map/triangular_solve/custom-call.0 | solution.py:20
  102.6 1.4 fusion.66
  104.0 3.2 fusion.2
  107.2 0.7 convolution_bitcast_fusion.8
  108.0 3.4 %collective-permute-start = (f32[1024,128]{0,1:T(8,128)S(1)}, f32[1024,128]{0,1:T(8,128)S(1)}, u32[]{:S(2)}, u32[]{:S(2)}) collective-permute-start(f32[1024,128]{0,1:T(8,128)S(1)} %pad_maximum_fusion.4), channel_id=1, source_target_pairs={{0,1},{1,0},{2,3},{3,2},{4,5},{5,4},{6,7},{7,6},{8,9},{9,8},{10,11... | collective-permute-start | bytes 1572872 | tf_op jit(solution)/shard_map/ppermute | solution.py:8
  111.4 11.7 %collective-permute-done = f32[1024,128]{0,1:T(8,128)S(1)} collective-permute-done((f32[1024,128]{0,1:T(8,128)S(1)}, f32[1024,128]{0,1:T(8,128)S(1)}, u32[]{:S(2)}, u32[]{:S(2)}) %collective-permute-start) | collective-permute-done | bytes 524320 | tf_op jit(solution)/shard_map/ppermute | solution.py:8
  123.1 1.1 select_bitcast_fusion.7
  124.2 0.9 fusion.36
  125.5 1.0 select_reduce_fusion.4
  127.2 5.8 %cholesky.100 = f32[64,64]{1,0:T(8,128)S(1)} custom-call(f32[64,64]{1,0:T(8,128)S(1)} %fusion.65), custom_call_target="Cholesky" | custom-call | tf_op jit(solution)/shard_map/jit(cholesky)/cholesky | solution.py:19
  134.4 4.9 %custom-call.10 = f32[1,64,64]{1,2,0:T(8,128)S(1)} custom-call(f32[1,64,64]{2,1,0:T(8,128)S(1)} %fusion.50), custom_call_target="InvertDiagBlocksLowerTriangular" | custom-call | tf_op jit(solution)/shard_map/triangular_solve/custom-call.0 | solution.py:20
  139.7 0.9 fusion.27
  141.1 4.2 %collective-permute-start.1 = (f32[1024,128]{0,1:T(8,128)S(1)}, f32[1024,128]{0,1:T(8,128)S(1)}, u32[]{:S(2)}, u32[]{:S(2)}) collective-permute-start(f32[1024,128]{0,1:T(8,128)S(1)} %pad_maximum_fusion.5), channel_id=1, source_target_pairs={{0,2},{1,3},{2,0},{3,1},{4,6},{5,7},{6,4},{7,5},{8,10},{9,11},{10,... | collective-permute-start | bytes 1572872 | tf_op jit(solution)/shard_map/ppermute | solution.py:8
  145.3 22.7 %collective-permute-done.1 = f32[1024,128]{0,1:T(8,128)S(1)} collective-permute-done((f32[1024,128]{0,1:T(8,128)S(1)}, f32[1024,128]{0,1:T(8,128)S(1)}, u32[]{:S(2)}, u32[]{:S(2)}) %collective-permute-start.1) | collective-permute-done | bytes 524320 | tf_op jit(solution)/shard_map/ppermute | solution.py:8
  168.1 0.9 fusion.34
  169.4 1.0 select_reduce_fusion.3
  171.2 5.8 %cholesky.111 = f32[64,64]{1,0:T(8,128)S(1)} custom-call(f32[64,64]{1,0:T(8,128)S(1)} %fusion.62), custom_call_target="Cholesky" | custom-call | tf_op jit(solution)/shard_map/jit(cholesky)/cholesky | solution.py:19
  177.7 0.7 fusion.51
  178.4 4.9 %custom-call.11 = f32[1,64,64]{1,2,0:T(8,128)S(1)} custom-call(f32[1,64,64]{2,1,0:T(8,128)S(1)} %fusion.51), custom_call_target="InvertDiagBlocksLowerTriangular" | custom-call | tf_op jit(solution)/shard_map/triangular_solve/custom-call.0 | solution.py:20
  183.7 0.9 fusion.25
  185.1 7.6 %collective-permute-start.2 = (f32[1024,128]{0,1:T(8,128)S(1)}, f32[1024,128]{0,1:T(8,128)S(1)}, u32[]{:S(2)}, u32[]{:S(2)}) collective-permute-start(f32[1024,128]{0,1:T(8,128)S(1)} %pad_maximum_fusion.6), channel_id=1, source_target_pairs={{0,4},{1,5},{2,6},{3,7},{4,0},{5,1},{6,2},{7,3},{8,12},{9,13},{10,... | collective-permute-start | bytes 1572872 | tf_op jit(solution)/shard_map/ppermute | solution.py:8
  192.7 44.8 %collective-permute-done.2 = f32[1024,128]{0,1:T(8,128)S(1)} collective-permute-done((f32[1024,128]{0,1:T(8,128)S(1)}, f32[1024,128]{0,1:T(8,128)S(1)}, u32[]{:S(2)}, u32[]{:S(2)}) %collective-permute-start.2) | collective-permute-done | bytes 524320 | tf_op jit(solution)/shard_map/ppermute | solution.py:8
  237.6 0.9 fusion.32
  239.0 1.0 select_reduce_fusion.2
  240.7 5.8 %cholesky.122 = f32[64,64]{1,0:T(8,128)S(1)} custom-call(f32[64,64]{1,0:T(8,128)S(1)} %fusion.59), custom_call_target="Cholesky" | custom-call | tf_op jit(solution)/shard_map/jit(cholesky)/cholesky | solution.py:19
  247.9 4.9 %custom-call.12 = f32[1,64,64]{1,2,0:T(8,128)S(1)} custom-call(f32[1,64,64]{2,1,0:T(8,128)S(1)} %fusion.52), custom_call_target="InvertDiagBlocksLowerTriangular" | custom-call | tf_op jit(solution)/shard_map/triangular_solve/custom-call.0 | solution.py:20
  253.2 0.9 fusion.23
  254.6 11.1 %collective-permute-start.3 = (f32[1024,128]{0,1:T(8,128)S(1)}, f32[1024,128]{0,1:T(8,128)S(1)}, u32[]{:S(2)}, u32[]{:S(2)}) collective-permute-start(f32[1024,128]{0,1:T(8,128)S(1)} %pad_maximum_fusion.7), channel_id=1, source_target_pairs={{0,8},{1,9},{2,10},{3,11},{4,12},{5,13},{6,14},{7,15},{8,0},{9,1},... | collective-permute-start | bytes 1572872 | tf_op jit(solution)/shard_map/ppermute | solution.py:8
  265.7 38.4 %collective-permute-done.3 = f32[1024,128]{0,1:T(8,128)S(1)} collective-permute-done((f32[1024,128]{0,1:T(8,128)S(1)}, f32[1024,128]{0,1:T(8,128)S(1)}, u32[]{:S(2)}, u32[]{:S(2)}) %collective-permute-start.3) | collective-permute-done | bytes 524320 | tf_op jit(solution)/shard_map/ppermute | solution.py:8
  304.2 0.9 fusion.30
  305.6 1.0 select_reduce_fusion.1
  307.3 5.8 %cholesky.133 = f32[64,64]{1,0:T(8,128)S(1)} custom-call(f32[64,64]{1,0:T(8,128)S(1)} %fusion.56), custom_call_target="Cholesky" | custom-call | tf_op jit(solution)/shard_map/jit(cholesky)/cholesky | solution.py:19
  314.5 4.9 %custom-call.13 = f32[1,64,64]{1,2,0:T(8,128)S(1)} custom-call(f32[1,64,64]{2,1,0:T(8,128)S(1)} %fusion.53), custom_call_target="InvertDiagBlocksLowerTriangular" | custom-call | tf_op jit(solution)/shard_map/triangular_solve/custom-call.0 | solution.py:20
  319.8 0.9 fusion.21
  321.2 0.7 copy.70
  (60 shorter events, 11.7 us)
Async XLA Ops:
  6.5 78.3 %copy-start = (f32[64,1024]{1,0:T(8,128)S(1)}, f32[64,1024]{1,0:T(8,128)}, u32[]{:S(2)}) copy-start(f32[64,1024]{1,0:T(8,128)} %param.10) | copy-start | bytes 786436
  6.5 68.5 %all-gather.2.cloned.1.call-start = ((), (), s32[]{:S(2)}) async-start(), calls=%async_computation | async-start | bytes 2162688 | tf_op jit(solution)/shard_map/all_gather | solution.py:35
  8.1 2.9 copy-start.4
  11.0 68.4 %copy-start.1 = (bf16[1,8,1024,128]{2,3,1,0:T(8,128)(2,1)}, bf16[1,8,1024,128]{2,3,1,0:T(8,128)(2,1)S(1)}, u32[]{:S(2)}) copy-start(bf16[1,8,1024,128]{2,3,1,0:T(8,128)(2,1)S(1)} %copy.40) | copy-start | bytes 6291460
  88.1 0.7 copy-start.2
  104.0 4.0 %copy-start.3 = (f32[64,1024]{1,0:T(8,128)}, f32[64,1024]{1,0:T(8,128)S(1)}, u32[]{:S(2)}) copy-start(f32[64,1024]{1,0:T(8,128)S(1)} %fusion.66) | copy-start | bytes 786436
  108.0 15.1 %collective-permute-start = (f32[1024,128]{0,1:T(8,128)S(1)}, f32[1024,128]{0,1:T(8,128)S(1)}, u32[]{:S(2)}, u32[]{:S(2)}) collective-permute-start(f32[1024,128]{0,1:T(8,128)S(1)} %pad_maximum_fusion.4), channel_id=1, source_target_pairs={{0,1},{1,0},{2,3},{3,2},{4,5},{5,4},{6,7},{7,6},{8,9},{9,8},{10,11... | collective-permute-start | bytes 1572872 | tf_op jit(solution)/shard_map/ppermute | solution.py:8
  141.1 26.9 %collective-permute-start.1 = (f32[1024,128]{0,1:T(8,128)S(1)}, f32[1024,128]{0,1:T(8,128)S(1)}, u32[]{:S(2)}, u32[]{:S(2)}) collective-permute-start(f32[1024,128]{0,1:T(8,128)S(1)} %pad_maximum_fusion.5), channel_id=1, source_target_pairs={{0,2},{1,3},{2,0},{3,1},{4,6},{5,7},{6,4},{7,5},{8,10},{9,11},{10,... | collective-permute-start | bytes 1572872 | tf_op jit(solution)/shard_map/ppermute | solution.py:8
  185.1 52.5 %collective-permute-start.2 = (f32[1024,128]{0,1:T(8,128)S(1)}, f32[1024,128]{0,1:T(8,128)S(1)}, u32[]{:S(2)}, u32[]{:S(2)}) collective-permute-start(f32[1024,128]{0,1:T(8,128)S(1)} %pad_maximum_fusion.6), channel_id=1, source_target_pairs={{0,4},{1,5},{2,6},{3,7},{4,0},{5,1},{6,2},{7,3},{8,12},{9,13},{10,... | collective-permute-start | bytes 1572872 | tf_op jit(solution)/shard_map/ppermute | solution.py:8
  254.6 49.5 %collective-permute-start.3 = (f32[1024,128]{0,1:T(8,128)S(1)}, f32[1024,128]{0,1:T(8,128)S(1)}, u32[]{:S(2)}, u32[]{:S(2)}) collective-permute-start(f32[1024,128]{0,1:T(8,128)S(1)} %pad_maximum_fusion.7), channel_id=1, source_target_pairs={{0,8},{1,9},{2,10},{3,11},{4,12},{5,13},{6,14},{7,15},{8,0},{9,1},... | collective-permute-start | bytes 1572872 | tf_op jit(solution)/shard_map/ppermute | solution.py:8
Sparse Core Ops, SparseCore 0:
  10.5 64.5 all-gather.1
where the time goes:
time: 329 us
  waiting for transfers between devices  182 us (55%)
  other arithmetic  62.1 us (19%)
  matrix products  28.6 us (9%)
  starting transfers between devices  26.3 us (8%)
  between operations  17.1 us (5%)
  local copies, waits for them, and re-layouts  13 us (4%)
    ppermute x4, waiting for transfers between devices, from_partner(): lax.ppermute(shard, axis, [(i, i ^ 1 << stride) for i in range(lax.axis_s...  118 us
    all_gather x1, waiting for transfers between devices, body(): panel = lax.all_gather(panel_factors, 'rows', axis=1, tiled=True)  64 us
    another operation x15, other arithmetic, compress(): chol = jnp.linalg.cholesky(gram)  32.6 us
    another operation x10, other arithmetic, compress(): lax.linalg.triangular_solve(chol, span, left_side=False, lower=True, tran...  27.7 us
    ppermute x4, starting transfers between devices, from_partner(): lax.ppermute(shard, axis, [(i, i ^ 1 << stride) for i in range(lax.axis_s...  26.3 us
    unnamed x13, local copies, waits for them, and re-layouts  7.62 us
    dot_general x5, matrix products, compress(): coef = jnp.einsum('nbr,bs->nrs', lefts, basis, precision=hi)  6.75 us
  transfers between devices with their start and end apart: 5, of which 5 were waited for; matrix products, arithmetic and copies ran while one was open for 1% of the time, Pallas kernels for 0%

commit v1 on v0

v1 whole, which is shorter than its diff:
```python
import jax
import jax.numpy as jnp
from jax import lax
from jax.experimental import pallas as pl
from jax.experimental.pallas import tpu as pltpu
from jax.sharding import PartitionSpec as P


F32 = jnp.float32
BF16 = jnp.bfloat16
R = 64
NN = (((1,), (0,)), ((), ()))
NT = (((1,), (1,)), ((), ()))
TN = (((0,), (0,)), ((), ()))
VMEM = pl.BlockSpec(memory_space=pltpu.VMEM)
SMEM = pl.BlockSpec(memory_space=pltpu.SMEM)


def mm(a, b, dims=NN):
    return lax.dot_general(a, b, dims, preferred_element_type=F32)


def split(x):
    hi = x.astype(BF16)
    return hi, (x - hi.astype(F32)).astype(BF16)


def dot3(a, b, dims=NN):
    ah, al = split(a)
    bh, bl = split(b)
    return mm(ah, bh, dims) + (mm(ah, bl, dims) + mm(al, bh, dims))


def eye_mask():
    r = lax.broadcasted_iota(jnp.int32, (R, R), 0)
    c = lax.broadcasted_iota(jnp.int32, (R, R), 1)
    return r == c


def shift_of(gram, diag):
    t = jnp.sum(jnp.where(diag, gram, 0.0), axis=1, keepdims=True)
    t = jnp.sum(t, axis=0, keepdims=True)
    return (0.001 / R) * t + 1e-20


def eliminate(mats, chol=False):
    n, wide = R // 8, (8, 2 * R)
    eye = jnp.where(eye_mask(), 1.0, 0.0).astype(F32)
    blocks = []
    for m in mats:
        aug = jnp.concatenate([eye, m], axis=1)
        blocks.append([aug[8 * i : 8 * i + 8, :] for i in range(n)])
    sub = lax.broadcasted_iota(jnp.int32, wide, 0)
    done = [[None] * n for _ in mats]

    def splat(v):
        return jnp.broadcast_to(v, wide)

    for j in range(0, R, 4):
        jb, js = j // 8, j % 8
        for blk, out in zip(blocks, done):
            r0, r1, r2, r3 = [splat(blk[jb][js + a : js + a + 1, :]) for a in range(4)]

            def at(row, b):
                return splat(row[:, R + j + b : R + j + b + 1])

            p00, p01, p02, p03 = [at(r0, b) for b in range(4)]
            p11, p12, p13 = [at(r1, b) for b in range(1, 4)]
            p22, p23, p33 = at(r2, 2), at(r2, 3), at(r3, 3)
            i1 = 1.0 / (p00 * p11 - p01 * p01)
            a00, a01, a11 = p11 * i1, -p01 * i1, p00 * i1
            t00, t01 = a00 * p02 + a01 * p12, a00 * p03 + a01 * p13
            t10, t11 = a01 * p02 + a11 * p12, a01 * p03 + a11 * p13
            s22 = p22 - (p02 * t00 + p12 * t10)
            s23 = p23 - (p02 * t01 + p12 * t11)
            s33 = p33 - (p03 * t01 + p13 * t11)
            i2 = 1.0 / (s22 * s33 - s23 * s23)
            z2 = r2 - (t00 * r0 + t10 * r1)
            z3 = r3 - (t01 * r0 + t11 * r1)
            q2 = (s33 * i2) * z2 - (s23 * i2) * z3
            q3 = (s22 * i2) * z3 - (s23 * i2) * z2
            q0 = (a00 * r0 + a01 * r1) - (t00 * q2 + t01 * q3)
            q1 = (a01 * r0 + a11 * r1) - (t10 * q2 + t11 * q3)
            for i in range(jb, n):
                if i == jb and js == 4:
                    continue
                c = [splat(blk[i][:, R + j + t : R + j + t + 1]) for t in range(4)]
                up = (c[0] * q0 + c[1] * q1) + (c[2] * q2 + c[3] * q3)
                blk[i] = blk[i] - (jnp.where(sub >= 4, up, 0.0) if i == jb else up)
            if chol:
                g0 = lax.rsqrt(p00)
                l1 = p01 * g0
                w0 = r0 * g0
                g1 = lax.rsqrt(p11 - l1 * l1)
                w1 = (r1 - l1 * w0) * g1
                ratio = s23 / s22
                w2 = z2 * lax.rsqrt(s22)
                w3 = (z3 - ratio * z2) * lax.rsqrt(s33 - s23 * ratio)
                keep = (w0, w1, w2, w3)
            else:
                keep = (q0, q1, q2, q3)
            acc = out[jb] if js else jnp.zeros(wide, F32)
            for t in range(4):
                acc = jnp.where(sub == js + t, keep[t], acc)
            out[jb] = acc
    res = []
    for blk, out in zip(blocks, done):
        rows = jnp.concatenate(out, axis=0)[:, :R]
        res.append(rows if chol else dot3(jnp.concatenate(blk, axis=0)[:, :R], rows, TN))
    return res


def inverses(grams):
    diag = eye_mask()
    shifts = [shift_of(g, diag) for g in grams]
    mats = [jnp.where(diag, g * (1.0 / s) + 1.0, g * (1.0 / s)) for g, s in zip(grams, shifts)]
    return shifts, eliminate(mats)


def ident():
    return jnp.where(eye_mask(), 1.0, 0.0).astype(F32)


def place():
    core, z = lax.axis_index("rows") % 2, lax.axis_index("upd")
    g = z // 4
    o = 2 - (g + core) % 2
    return core, z, g, o, 2 * o - 3


def interleave(core, own_ref, oth_ref, pan):
    for c in range(16):
        pan[:, c, pl.ds(core, 1), :, :] = own_ref[c][:, None]
        pan[:, c, pl.ds(1 - core, 1), :, :] = oth_ref[c][:, None]


def leaf_y(w_ref, tile_ref, own_ref, oth_ref, sk_ref, y_ref, inner_ref, pan):
    core = place()[0]
    interleave(core, own_ref, oth_ref, pan)
    sh, sl = split(sk_ref[...])
    r = lax.broadcasted_iota(jnp.int32, (R, 2 * R), 0)
    c = lax.broadcasted_iota(jnp.int32, (R, 2 * R), 1)
    pick = jnp.where(c == r + R, 1.0, 0.0).astype(BF16)
    zero = jnp.zeros((R, R), F32)
    acc = jnp.zeros((R, 1024), F32)
    for k in range(8):
        tile = tile_ref[k]
        pan_k = pan[k].reshape(1024, 2 * R)
        vt = mm(pick, tile, NT).astype(BF16)
        res = mm(jnp.concatenate([sh, sl, vt], axis=0), pan_k)
        proj = (res[:R] + res[R : 2 * R])[:, :R]
        inner = res[2 * R :][:, R:] * w_ref[k].astype(F32)
        inner_ref[k] = inner
        dt = jnp.concatenate([dot3(proj, inner, NT), zero], axis=1)
        dh, dl = split(dt)
        out = mm(jnp.concatenate([dh, dl], axis=0), tile, NT)
        acc = acc + (out[:R] + out[R:])
    y_ref[...] = acc


def leaf_x(tile_ref, own_ref, oth_ref, y_ref, inner_ref, x_ref, pan):
    core = place()[0]
    interleave(core, own_ref, oth_ref, pan)
    yh, yl = split(y_ref[...])
    ys = jnp.concatenate([yh, yl], axis=0)
    zero = jnp.zeros((R, R), F32)
    acc = jnp.zeros((R, 1024), F32)
    for k in range(8):
        pan_k = pan[k].reshape(1024, 2 * R)
        ht = mm(ys, tile_ref[k])
        ht = (ht[:R] + ht[R:])[:, :R]
        et = jnp.concatenate([dot3(ht, inner_ref[k]), zero], axis=1)
        eh, el = split(et)
        out = mm(jnp.concatenate([eh, el], axis=0), pan_k, NT)
        acc = acc + (out[:R] + out[R:])
    x_ref[...] = acc


def lanes(mats):
    return jnp.concatenate(mats, axis=1)


def rows_of(mats):
    return jnp.concatenate(mats, axis=0)


def put_shift(s):
    return jnp.broadcast_to(s, (8, 2 * R))


def group_y(y0, y1, y2, y3, out_ref, k_ref, j_ref, s_ref):
    stack = rows_of([y0[...], y1[...], y2[...], y3[...]])
    ah, al = split(stack)
    gram = mm(ah, ah, NT) + (mm(ah, al, NT) + mm(al, ah, NT))
    k_ref[...] = gram
    eye = ident()
    shifts, js = inverses([gram[R * u : R * u + R, R * u : R * u + R] for u in range(4)])
    rs = [eye - j for j in js]
    pair_r = [lanes(rs[0:2]), lanes(rs[2:4])]
    grams = []
    for m in range(2):
        kp = gram[2 * R * m : 2 * R * m + 2 * R, 2 * R * m : 2 * R * m + 2 * R]
        grams.append(dot3(dot3(pair_r[m], kp), rows_of(rs[2 * m : 2 * m + 2])))
    shifts2, js2 = inverses(grams)
    pt = lanes([dot3(eye - js2[m], pair_r[m]) for m in range(2)])
    ph, plo = split(pt)
    out_ref[...] = mm(ph, ah) + (mm(ph, al) + mm(plo, ah))
    for u, j in enumerate(js + js2):
        j_ref[u] = j
    for u, s in enumerate(shifts + shifts2):
        s_ref[u] = put_shift(1.0 / s)


def group_x(x0, x1, x2, x3, k_ref, j_ref, s_ref, send_ref, keep_ref):
    eye = ident()
    gram = k_ref[...]
    js = [j_ref[u] for u in range(6)]
    ss = [s_ref[u][:1, :1] for u in range(6)]
    rs = [eye - j for j in js]
    pt, q1 = [], []
    for m in range(2):
        pr = lanes(rs[2 * m : 2 * m + 2])
        kp = gram[2 * R * m : 2 * R * m + 2 * R, 2 * R * m : 2 * R * m + 2 * R]
        rk = dot3(pr, kp)
        q1.append(
            lanes([dot3(rk[:, :R] * ss[2 * m], js[2 * m]), dot3(rk[:, R:] * ss[2 * m + 1], js[2 * m + 1])])
        )
        pt.append(dot3(rs[4 + m], pr))
    pk = dot3(lanes(pt), gram)
    qt = []
    for m in range(2):
        t = dot3(pk[:, 2 * R * m : 2 * R * m + 2 * R], rows_of(rs[2 * m : 2 * m + 2]))
        t = dot3(t * ss[4 + m], js[4 + m])
        qt.append(dot3(t, q1[m]))
    qh, ql = split(lanes(qt))
    refs = (x0, x1, x2, x3)
    g = place()[2]
    sib = g + 1 - 2 * (g % 2)
    for dst, blocks in ((send_ref, (sib, 3 - sib)), (keep_ref, (g, 3 - g))):
        for i, block in enumerate(blocks):
            at = pl.multiple_of(block * 256, 256)
            xh, xl = split(rows_of([x[:, pl.ds(at, 256)] for x in refs]))
            dst[:, 256 * i : 256 * i + 256] = mm(qh, xh) + (mm(qh, xl) + mm(ql, xh))


def merge_y(y0, y1, out_ref, k_ref, j_ref, s_ref):
    ah, al = split(rows_of([y0[...], y1[...]]))
    gram = mm(ah, ah, NT) + (mm(ah, al, NT) + mm(al, ah, NT))
    k_ref[...] = gram
    eye = ident()
    shifts, js = inverses([gram[R * u : R * u + R, R * u : R * u + R] for u in range(2)])
    ph, plo = split(lanes([eye - j for j in js]))
    out_ref[...] = mm(ph, ah) + (mm(ph, al) + mm(plo, ah))
    for u in range(2):
        j_ref[u] = js[u]
        s_ref[u] = put_shift(1.0 / shifts[u])


def merge_q(gram, js, ss):
    eye = ident()
    rk = dot3(lanes([eye - j for j in js]), gram)
    return lanes([dot3(rk[:, R * u : R * u + R] * ss[u], js[u]) for u in range(2)])


def merge_x(x0, x1, k_ref, j_ref, s_ref, send_ref, keep_ref):
    qt = merge_q(k_ref[...], [j_ref[u] for u in range(2)], [s_ref[u][:1, :1] for u in range(2)])
    out = dot3(qt, rows_of([x0[...], x1[...]]))
    keep_ref[...] = out[:, :256]
    send_ref[...] = out[:, 256:]


def root_y(y0, y1, w_ref, f_ref):
    ah, al = split(rows_of([y0[...], y1[...]]))
    gram = mm(ah, ah, NT) + (mm(ah, al, NT) + mm(al, ah, NT))
    eye = ident()
    shifts, js = inverses([gram[R * u : R * u + R, R * u : R * u + R] for u in range(2)])
    rs = [eye - j for j in js]
    pr = lanes(rs)
    g = dot3(dot3(pr, gram), rows_of(rs))
    diag = eye_mask()
    s = shift_of(g, diag)
    rec = 1.0 / s
    (ci,) = eliminate([jnp.where(diag, g * rec + 1.0, g * rec)], chol=True)
    ci = ci * lax.rsqrt(s)
    f_ref[...] = dot3(ci, merge_q(gram, js, [1.0 / v for v in shifts]))
    at = pl.multiple_of(place()[2] * 256, 256)
    yr = rows_of([y0[:, pl.ds(at, 256)], y1[:, pl.ds(at, 256)]])
    w_ref[...] = dot3(dot3(ci, pr), yr) * 32.0


def root_out(w_ref, f_ref, x0, x1, o0, o1, o2, o3, buf):
    zt = dot3(f_ref[...], rows_of([x0[...], x1[...]])) * (1.0 / 32.0)
    buf[...] = rows_of([w_ref[...], zt]).T
    _, z, g, o, e = place()
    mine = jnp.where(z == 4 * g + o, 1, 0)

    def block(j):
        return buf[pl.ds(pl.multiple_of(j * R, R), R), :]

    o0[...] = jnp.where(jnp.full((R, 2 * R), mine) == 1, block(o), 0.0)
    o1[...], o2[...], o3[...] = block(o + e), block(o - e), block(o - 2 * e)


def shape(*dims, dtype=F32):
    return jax.ShapeDtypeStruct(dims, dtype)


def call(fn, outs, n_smem, args, scratch=(), flops=10**8):
    specs = [SMEM] * n_smem + [VMEM] * (len(args) - n_smem)
    many = isinstance(outs, (tuple, list))
    kernel = pl.pallas_call(
        fn,
        out_shape=outs,
        in_specs=specs,
        out_specs=[VMEM] * len(outs) if many else VMEM,
        scratch_shapes=list(scratch),
        cost_estimate=pl.CostEstimate(flops=flops, bytes_accessed=10**6, transcendentals=0),
        compiler_params=pltpu.CompilerParams(vmem_limit_bytes=20 * 2**20),
    )
    return kernel(*args)


OWNERS = ((2, 5, 10, 13), (1, 6, 9, 14))
SIDE = ((1, -1, 1, -1), (-1, 1, -1, 1))


def over_rows(per_core, rows, upd):
    return [(r * upd + a, r * upd + b) for r in range(rows) for a, b in per_core[r % 2]]


def tables(rows, upd):
    member = []
    for off in (1, -1, -2):
        member.append([[(o + off * e, o) for o, e in zip(OWNERS[c], SIDE[c])] for c in range(2)])
    third = [[(OWNERS[c][i], OWNERS[c][i ^ 1]) for i in range(4)] for c in range(2)]
    fourth = [[(OWNERS[c][i], OWNERS[c][3 - i]) for i in range(4)] for c in range(2)]
    back = [[[(b, a) for a, b in m[c]] for c in range(2)] for m in member]
    full = lambda p: over_rows(p, rows, upd)
    return [full(m) for m in member], full(third), full(fourth), [full(m) for m in back]


def tree(y, leaf_x_of, rows, upd):
    members, third, fourth, back = tables(rows, upd)

    def send(v, perm):
        return lax.ppermute(v, ("rows", "upd"), perm)

    ys = [y] + [send(y, m) for m in members]
    x = leaf_x_of(y)
    xs = [x] + [send(x, m) for m in members]
    sizes = (shape(R, 1024), shape(256, 256), shape(6, R, R), shape(6, 8, 128))
    y2, k2, j2, s2 = call(group_y, sizes, 0, ys)
    y2h = send(y2, third)
    xsend, xkeep = call(group_x, (shape(R, 512), shape(R, 512)), 0, [*xs, k2, j2, s2])
    xh = send(xsend, third)
    sizes = (shape(R, 1024), shape(128, 128), shape(2, R, R), shape(2, 8, 128))
    y3, k3, j3, s3 = call(merge_y, sizes, 0, [y2, y2h])
    y3h = send(y3, fourth)
    xsend, xkeep = call(merge_x, (shape(R, 256), shape(R, 256)), 0, [xkeep, xh, k3, j3, s3])
    xh = send(xsend, fourth)
    wt, f = call(root_y, (shape(R, 256), shape(R, 128)), 0, [y3, y3h])
    buf = [pltpu.VMEM((256, 128), F32)]
    outs = call(root_out, [shape(R, 128)] * 4, 0, [wt, f, xkeep, xh], scratch=buf)
    res = outs[0]
    for o, p in zip(outs[1:], back):
        res = res + send(o, p)
    return res


def local_update(tiles, own, oth, nonnull, sketch, rows, upd):
    pan = pltpu.VMEM((8, 16, 2, 32, 128), BF16)
    tiles = tiles.reshape(8, 1024, 2 * R)
    y, inner = call(
        leaf_y, (shape(R, 1024), shape(8, R, R)), 1, [nonnull, tiles, own, oth, sketch], scratch=[pan]
    )

    def leaf_x_of(y):
        return call(leaf_x, shape(R, 1024), 0, [tiles, own, oth, y, inner], scratch=[pan])

    return tree(y, leaf_x_of, rows, upd)


def body(tile_factors, panel_factors, nonnull, sketch):
    rows, upd = lax.axis_size("rows"), lax.axis_size("upd")
    same = [[2 * i + c for i in range(rows // 2)] for c in range(2)]
    blocks = jnp.broadcast_to(panel_factors[None], (rows // 2,) + panel_factors.shape)
    own = lax.all_to_all(blocks, "rows", 0, 0, axis_index_groups=same)
    oth = lax.ppermute(own, "rows", [(i, i ^ 1) for i in range(rows)])
    return local_update(tile_factors[0], own, oth, nonnull[0], sketch, rows, upd)[None]


def solution(mesh):
    in_specs = (P("rows", "upd", None, None), P("upd", "rows", None), P("rows", "upd"), P())
    out_specs = P("rows", "upd", None)
    return jax.shard_map(body, mesh=mesh, in_specs=in_specs, out_specs=out_specs, check_vma=False)
```

time: 329 us -> 120 us (0.36)
  waiting for transfers between devices: 182 us -> 28.3 us
  other arithmetic: 62.1 us -> 0.63 us
  Pallas kernels: 0 us -> 34.4 us
  matrix products: 28.6 us -> 0 us
  blocking collectives: 0 us -> 22.4 us
  between operations: 17.1 us -> 0.26 us
  local copies, waits for them, and re-layouts: 13 us -> 1.2 us
  starting transfers between devices: 26.3 us -> 30.9 us
    ppermute x4 -> x14, waiting for transfers between devices: 118 us -> 28.3 us  [the longest x13 26 us: send(): return lax.ppermute(v, ('rows', 'upd'), perm)]
    all_gather x1 -> x0, waiting for transfers between devices: 64 us -> none  [body(): panel = lax.all_gather(panel_factors, 'rows', axis=1, tiled=True)]
    another operation x29 -> x0, other arithmetic: 61.7 us -> none  [the longest x15 32.6 us: compress(): chol = jnp.linalg.cholesky(gram)]
    pallas_call x0 -> x8, Pallas kernels: none -> 34.4 us  [call(): return kernel(*args)]
    dot_general x27 -> x0, matrix products: 25.5 us -> none  [the longest x5 6.75 us: compress(): coef = jnp.einsum('nbr,bs->nrs', lefts, basis, precision=hi)]
    all_to_all x0 -> x1, blocking collectives: none -> 22.4 us  [body(): own = lax.all_to_all(blocks, 'rows', 0, 0, axis_index_groups=same)]
    unnamed x13 -> x6, local copies, waits for them, and re-layouts: 7.62 us -> 0.01 us
    ppermute x4 -> x14, starting transfers between devices: 26.3 us -> 30.9 us  [the longest x13 26 us: send(): return lax.ppermute(v, ('rows', 'upd'), perm)]
  transfers between devices with their start and end apart: 5 -> 14, of which waited for: 5 -> 3; matrix products, arithmetic and copies ran while one was open for 1% -> 0% of each run, Pallas kernels for 0% -> 16%
where the time goes in v1:
time: 120 us; the launch traced here: 118 us
  Pallas kernels  34.4 us (29%)
  starting transfers between devices  30.9 us (26%)
  waiting for transfers between devices  28.3 us (24%)
  blocking collectives  22.4 us (19%)
  local copies, waits for them, and re-layouts  1.2 us (1%)
    pallas_call x8, Pallas kernels, call(): return kernel(*args)  34.4 us
    ppermute x13, waiting for transfers between devices, send(): return lax.ppermute(v, ('rows', 'upd'), perm)  26 us
    ppermute x13, starting transfers between devices, send(): return lax.ppermute(v, ('rows', 'upd'), perm)  26 us
    all_to_all x1, blocking collectives, body(): own = lax.all_to_all(blocks, 'rows', 0, 0, axis_index_groups=same)  22.4 us
    ppermute x1, starting transfers between devices, body(): oth = lax.ppermute(own, 'rows', [(i, i ^ 1) for i in range(rows)])  4.96 us
  transfers between devices with their start and end apart: 14, of which 3 were waited for; matrix products, arithmetic and copies ran while one was open for 0% of the time, Pallas kernels for 16%

profile of v1, /device:TPU:1, one launch (start us, length us, event | category | flops | bytes accessed | tf_op | source)
XLA Modules:
  0.0 118.1 jit_solution(14757749901608868807)
XLA Ops:
  0.0 0.0 copy-start.1
  0.0 0.0 copy-start.2
  0.0 0.0 copy-start
  0.0 1.2 %broadcast_in_dim.4 = bf16[16,8,32,128]{3,2,1,0:T(8,128)(2,1)S(1)} broadcast(bf16[8,32,128]{2,1,0:T(8,128)(2,1)} %param.5), dimensions={1,2,3} | broadcast | bytes 1114112 | tf_op jit(solution)/shard_map/broadcast_in_dim | solution.py:386
  1.2 22.4 %all_to_all.5.own_ref = bf16[16,8,32,128]{3,2,1,0:T(8,128)(2,1)S(1)} all-to-all(bf16[16,8,32,128]{3,2,1,0:T(8,128)(2,1)S(1)} %broadcast_in_dim.4), channel_id=1, replica_groups={{0,32,64,96,128,160,192,224,256,288,320,352,384,416,448,480},{16,48,80,..., dimensions={0} | all-to-all | bytes 2097152 | tf_op jit(solution)/shard_map/all_to_all | solution.py:387
  23.6 5.0 %collective-permute-start = (bf16[16,8,32,128]{3,2,1,0:T(8,128)(2,1)S(1)}, bf16[16,8,32,128]{3,2,1,0:T(8,128)(2,1)S(1)}, u32[]{:S(2)}, u32[]{:S(2)}) collective-permute-start(bf16[16,8,32,128]{3,2,1,0:T(8,128)(2,1)S(1)} %all_to_all.5.own_ref), channel_id=1, source_target_pairs={{0,16},{16,0},{32,48},{48,32},{64,80},{80,64},{96,112},{112,96},{1... | collective-permute-start | bytes 3145736 | tf_op jit(solution)/shard_map/ppermute | solution.py:388
  28.5 2.3 %collective-permute-done.oth_ref = bf16[16,8,32,128]{3,2,1,0:T(8,128)(2,1)S(1)} collective-permute-done((bf16[16,8,32,128]{3,2,1,0:T(8,128)(2,1)S(1)}, bf16[16,8,32,128]{3,2,1,0:T(8,128)(2,1)S(1)}, u32[]{:S(2)}, u32[]{:S(2)}) %collective-permute-start) | collective-permute-done | bytes 1048608 | tf_op jit(solution)/shard_map/ppermute | solution.py:388
  30.8 0.0 copy-done.1
  30.8 0.0 copy-done.2
  30.8 0.0 copy-done
  30.8 6.0 %shard_map.46 = (f32[64,1024]{1,0:T(8,128)S(1)}, f32[8,64,64]{2,1,0:T(8,128)S(1)}) custom-call(s32[8]{0:T(128)S(1)} %bitcast.6, bf16[8,1024,128]{2,1,0:T(8,128)(2,1)S(1)} %bitcast.4, bf16[16,8,32,128]{3,2,1,0:T(8,128)(2,1)S(1)} %all_to_all.5.own_ref, bf16[16,8,32,128]{3,2,1,0:T(8,128)(2,1)S(1)} %collective-permute-done.oth_ref, f32[64,1024]{1,0:T(8,128)S(1)} %copy-done.1), custom_call_target="tpu_custom_call" | custom-call | flops 100000000 | bytes 1000000 | tf_op jit(solution)/shard_map/pallas_call | solution.py:320
  36.8 0.7 collective-permute-start.3
  37.5 0.7 collective-permute-start.2
  38.2 4.5 %collective-permute-start.1 = (f32[64,1024]{1,0:T(8,128)S(1)}, f32[64,1024]{1,0:T(8,128)S(1)}, u32[]{:S(2)}, u32[]{:S(2)}) collective-permute-start(f32[64,1024]{1,0:T(8,128)S(1)} %get-tuple-element.25.y0.y_ref), channel_id=1, source_target_pairs={{3,2},{4,5},{11,10},{12,13},{16,17},{23,22},{24,25},{31,30},{35,34... | collective-permute-start | bytes 786440 | tf_op jit(solution)/shard_map/ppermute | solution.py:346
  42.7 0.0 collective-permute-done.3.y3
  42.7 0.0 collective-permute-done.2.y2
  42.7 5.7 %collective-permute-done.1.y1 = f32[64,1024]{1,0:T(8,128)S(1)} collective-permute-done((f32[64,1024]{1,0:T(8,128)S(1)}, f32[64,1024]{1,0:T(8,128)S(1)}, u32[]{:S(2)}, u32[]{:S(2)}) %collective-permute-start.1) | collective-permute-done | bytes 262176 | tf_op jit(solution)/shard_map/ppermute | solution.py:346
  48.4 9.8 %shard_map.47 = (f32[64,1024]{1,0:T(8,128)S(1)}, f32[256,256]{1,0:T(8,128)S(1)}, f32[6,64,64]{2,1,0:T(8,128)S(1)}, f32[6,8,128]{2,1,0:T(8,128)S(1)}) custom-call(f32[64,1024]{1,0:T(8,128)S(1)} %get-tuple-element.25.y0.y_ref, f32[64,1024]{1,0:T(8,128)S(1)} %collective-permute-done.1.y1, f32[64,1024]{1,0:T(8,128)S(1)} %collective-permute-done.2.y2, ...), custom_call_target="tpu_custom_call" | custom-call | flops 100000000 | bytes 1000000 | tf_op jit(solution)/shard_map/pallas_call | solution.py:320
  58.2 0.7 collective-permute-start.4
  58.9 3.5 %shard_map.50.x0 = f32[64,1024]{1,0:T(8,128)S(1)} custom-call(bf16[8,1024,128]{2,1,0:T(8,128)(2,1)S(1)} %bitcast.5, bf16[16,8,32,128]{3,2,1,0:T(8,128)(2,1)S(1)} %all_to_all.5.own_ref, bf16[16,8,32,128]{3,2,1,0:T(8,128)(2,1)S(1)} %collective-permute-done.oth_ref, f32[64,1024]{1,0:T(8,128)S(1)} %get-tuple-element.25.y0.y_ref, ...), custom_call_target="tpu_custom_call" | custom-call | flops 100000000 | bytes 1000000 | tf_op jit(solution)/shard_map/pallas_call | solution.py:320
  62.4 0.9 collective-permute-start.8
  63.3 0.7 collective-permute-start.7
  64.0 13.2 %collective-permute-start.6 = (f32[64,1024]{1,0:T(8,128)S(1)}, f32[64,1024]{1,0:T(8,128)S(1)}, u32[]{:S(2)}, u32[]{:S(2)}) collective-permute-start(f32[64,1024]{1,0:T(8,128)S(1)} %shard_map.50.x0), channel_id=1, source_target_pairs={{3,2},{4,5},{11,10},{12,13},{16,17},{23,22},{24,25},{31,30},{35,34... | collective-permute-start | bytes 786440 | tf_op jit(solution)/shard_map/ppermute | solution.py:346
  77.2 0.0 collective-permute-done.4.y1
  77.2 4.5 %shard_map.48 = (f32[64,1024]{1,0:T(8,128)S(1)}, f32[128,128]{1,0:T(8,128)S(1)}, f32[2,64,64]{2,1,0:T(8,128)S(1)}, f32[2,8,128]{2,1,0:T(8,128)S(1)}) custom-call(f32[64,1024]{1,0:T(8,128)S(1)} %get-tuple-element.26.y0, f32[64,1024]{1,0:T(8,128)S(1)} %collective-permute-done.4.y1), custom_call_target="tpu_custom_call" | custom-call | flops 100000000 | bytes 1000000 | tf_op jit(solution)/shard_map/pallas_call | solution.py:320
  81.7 0.7 collective-permute-start.5
  82.4 0.0 collective-permute-done.8.x3
  82.4 0.0 collective-permute-done.7.x2
  82.4 0.0 collective-permute-done.6.x1
  82.4 1.8 %shard_map.51 = (f32[64,512]{1,0:T(8,128)S(1)}, f32[64,512]{1,0:T(8,128)S(1)}) custom-call(f32[64,1024]{1,0:T(8,128)S(1)} %shard_map.50.x0, f32[64,1024]{1,0:T(8,128)S(1)} %collective-permute-done.6.x1, f32[64,1024]{1,0:T(8,128)S(1)} %collective-permute-done.7.x2, f32[64,1024]{1,0:T(8,128)S(1)} %collective-permute-done.8.x3, ...), custom_call_target="tpu_custom_call" | custom-call | flops 100000000 | bytes 1000000 | tf_op jit(solution)/shard_map/pallas_call | solution.py:320
  84.2 0.7 collective-permute-start.9
  84.9 0.0 collective-permute-done.9.x1
  84.9 0.7 shard_map.52
  85.6 0.7 collective-permute-start.10
  86.3 0.0 collective-permute-done.5.y1
  86.3 7.9 %shard_map.49 = (f32[64,256]{1,0:T(8,128)S(1)}, f32[64,128]{1,0:T(8,128)S(1)}) custom-call(f32[64,1024]{1,0:T(8,128)S(1)} %get-tuple-element.27.y0, f32[64,1024]{1,0:T(8,128)S(1)} %collective-permute-done.5.y1), custom_call_target="tpu_custom_call" | custom-call | flops 100000000 | bytes 1000000 | tf_op jit(solution)/shard_map/pallas_call | solution.py:320
  94.2 0.0 collective-permute-done.10.x1
  94.2 0.3 shard_map.53
  94.5 1.3 %collective-permute-start.11 = (f32[64,128]{1,0:T(8,128)S(1)}, f32[64,128]{1,0:T(8,128)S(1)}, u32[]{:S(2)}, u32[]{:S(2)}) collective-permute-start(f32[64,128]{1,0:T(8,128)S(1)} %get-tuple-element.42), channel_id=1, source_target_pairs={{2,3},{5,4},{10,11},{13,12},{17,16},{22,23},{25,24},{30,31},{34,35... | collective-permute-start | bytes 98312 | tf_op jit(solution)/shard_map/ppermute | solution.py:346
  95.8 0.7 collective-permute-start.12
  96.4 0.7 collective-permute-start.13
  97.1 20.3 %collective-permute-done.11 = f32[64,128]{1,0:T(8,128)S(1)} collective-permute-done((f32[64,128]{1,0:T(8,128)S(1)}, f32[64,128]{1,0:T(8,128)S(1)}, u32[]{:S(2)}, u32[]{:S(2)}) %collective-permute-start.11) | collective-permute-done | bytes 32800 | tf_op jit(solution)/shard_map/ppermute | solution.py:346
  117.4 0.0 collective-permute-done.12
  117.4 0.0 collective-permute-done.13
  117.4 0.6 add_bitcast_fusion
Async XLA Ops:
  0.0 30.8 %copy-start.1 = (f32[64,1024]{1,0:T(8,128)S(1)}, f32[64,1024]{1,0:T(8,128)}, u32[]{:S(2)}) copy-start(f32[64,1024]{1,0:T(8,128)} %sk_ref.1) | copy-start | bytes 786436
  0.0 30.8 %copy-start.2 = (s32[1,8]{1,0:T(1,128)S(1)}, s32[1,8]{1,0:T(1,128)}, u32[]{:S(2)}) copy-start(s32[1,8]{1,0:T(1,128)} %param.6) | copy-start | bytes 100
  0.0 30.8 %copy-start = (bf16[1,8,1024,128]{3,2,1,0:T(8,128)(2,1)S(1)}, bf16[1,8,1024,128]{3,2,1,0:T(8,128)(2,1)}, u32[]{:S(2)}) copy-start(bf16[1,8,1024,128]{3,2,1,0:T(8,128)(2,1)} %param.4) | copy-start | bytes 6291460
  23.6 7.2 %collective-permute-start = (bf16[16,8,32,128]{3,2,1,0:T(8,128)(2,1)S(1)}, bf16[16,8,32,128]{3,2,1,0:T(8,128)(2,1)S(1)}, u32[]{:S(2)}, u32[]{:S(2)}) collective-permute-start(bf16[16,8,32,128]{3,2,1,0:T(8,128)(2,1)S(1)} %all_to_all.5.own_ref), channel_id=1, source_target_pairs={{0,16},{16,0},{32,48},{48,32},{64,80},{80,64},{96,112},{112,96},{1... | collective-permute-start | bytes 3145736 | tf_op jit(solution)/shard_map/ppermute | solution.py:388
  36.8 5.9 %collective-permute-start.3 = (f32[64,1024]{1,0:T(8,128)S(1)}, f32[64,1024]{1,0:T(8,128)S(1)}, u32[]{:S(2)}, u32[]{:S(2)}) collective-permute-start(f32[64,1024]{1,0:T(8,128)S(1)} %get-tuple-element.25.y0.y_ref), channel_id=1, source_target_pairs={{0,2},{7,5},{8,10},{15,13},{19,17},{20,22},{27,25},{28,30},{32,34}... | collective-permute-start | bytes 786440 | tf_op jit(solution)/shard_map/ppermute | solution.py:346
  37.5 5.2 %collective-permute-start.2 = (f32[64,1024]{1,0:T(8,128)S(1)}, f32[64,1024]{1,0:T(8,128)S(1)}, u32[]{:S(2)}, u32[]{:S(2)}) collective-permute-start(f32[64,1024]{1,0:T(8,128)S(1)} %get-tuple-element.25.y0.y_ref), channel_id=1, source_target_pairs={{1,2},{6,5},{9,10},{14,13},{18,17},{21,22},{26,25},{29,30},{33,34}... | collective-permute-start | bytes 786440 | tf_op jit(solution)/shard_map/ppermute | solution.py:346
  38.2 10.2 %collective-permute-start.1 = (f32[64,1024]{1,0:T(8,128)S(1)}, f32[64,1024]{1,0:T(8,128)S(1)}, u32[]{:S(2)}, u32[]{:S(2)}) collective-permute-start(f32[64,1024]{1,0:T(8,128)S(1)} %get-tuple-element.25.y0.y_ref), channel_id=1, source_target_pairs={{3,2},{4,5},{11,10},{12,13},{16,17},{23,22},{24,25},{31,30},{35,34... | collective-permute-start | bytes 786440 | tf_op jit(solution)/shard_map/ppermute | solution.py:346
  58.2 19.0 %collective-permute-start.4 = (f32[64,1024]{1,0:T(8,128)S(1)}, f32[64,1024]{1,0:T(8,128)S(1)}, u32[]{:S(2)}, u32[]{:S(2)}) collective-permute-start(f32[64,1024]{1,0:T(8,128)S(1)} %get-tuple-element.26.y0), channel_id=1, source_target_pairs={{2,5},{5,2},{10,13},{13,10},{17,22},{22,17},{25,30},{30,25},{34,37... | collective-permute-start | bytes 786440 | tf_op jit(solution)/shard_map/ppermute | solution.py:346
  62.4 20.0 %collective-permute-start.8 = (f32[64,1024]{1,0:T(8,128)S(1)}, f32[64,1024]{1,0:T(8,128)S(1)}, u32[]{:S(2)}, u32[]{:S(2)}) collective-permute-start(f32[64,1024]{1,0:T(8,128)S(1)} %shard_map.50.x0), channel_id=1, source_target_pairs={{0,2},{7,5},{8,10},{15,13},{19,17},{20,22},{27,25},{28,30},{32,34}... | collective-permute-start | bytes 786440 | tf_op jit(solution)/shard_map/ppermute | solution.py:346
  63.3 19.1 %collective-permute-start.7 = (f32[64,1024]{1,0:T(8,128)S(1)}, f32[64,1024]{1,0:T(8,128)S(1)}, u32[]{:S(2)}, u32[]{:S(2)}) collective-permute-start(f32[64,1024]{1,0:T(8,128)S(1)} %shard_map.50.x0), channel_id=1, source_target_pairs={{1,2},{6,5},{9,10},{14,13},{18,17},{21,22},{26,25},{29,30},{33,34}... | collective-permute-start | bytes 786440 | tf_op jit(solution)/shard_map/ppermute | solution.py:346
  64.0 18.5 %collective-permute-start.6 = (f32[64,1024]{1,0:T(8,128)S(1)}, f32[64,1024]{1,0:T(8,128)S(1)}, u32[]{:S(2)}, u32[]{:S(2)}) collective-permute-start(f32[64,1024]{1,0:T(8,128)S(1)} %shard_map.50.x0), channel_id=1, source_target_pairs={{3,2},{4,5},{11,10},{12,13},{16,17},{23,22},{24,25},{31,30},{35,34... | collective-permute-start | bytes 786440 | tf_op jit(solution)/shard_map/ppermute | solution.py:346
  81.7 4.6 %collective-permute-start.5 = (f32[64,1024]{1,0:T(8,128)S(1)}, f32[64,1024]{1,0:T(8,128)S(1)}, u32[]{:S(2)}, u32[]{:S(2)}) collective-permute-start(f32[64,1024]{1,0:T(8,128)S(1)} %get-tuple-element.27.y0), channel_id=1, source_target_pairs={{2,13},{5,10},{10,5},{13,2},{17,30},{22,25},{25,22},{30,17},{34,45... | collective-permute-start | bytes 786440 | tf_op jit(solution)/shard_map/ppermute | solution.py:346
  84.2 0.7 collective-permute-start.9
  85.6 8.6 %collective-permute-start.10 = (f32[64,256]{1,0:T(8,128)S(1)}, f32[64,256]{1,0:T(8,128)S(1)}, u32[]{:S(2)}, u32[]{:S(2)}) collective-permute-start(f32[64,256]{1,0:T(8,128)S(1)} %get-tuple-element.40), channel_id=1, source_target_pairs={{2,13},{5,10},{10,5},{13,2},{17,30},{22,25},{25,22},{30,17},{34,45... | collective-permute-start | bytes 196616 | tf_op jit(solution)/shard_map/ppermute | solution.py:346
  94.5 23.0 %collective-permute-start.11 = (f32[64,128]{1,0:T(8,128)S(1)}, f32[64,128]{1,0:T(8,128)S(1)}, u32[]{:S(2)}, u32[]{:S(2)}) collective-permute-start(f32[64,128]{1,0:T(8,128)S(1)} %get-tuple-element.42), channel_id=1, source_target_pairs={{2,3},{5,4},{10,11},{13,12},{17,16},{22,23},{25,24},{30,31},{34,35... | collective-permute-start | bytes 98312 | tf_op jit(solution)/shard_map/ppermute | solution.py:346
  95.8 21.7 %collective-permute-start.12 = (f32[64,128]{1,0:T(8,128)S(1)}, f32[64,128]{1,0:T(8,128)S(1)}, u32[]{:S(2)}, u32[]{:S(2)}) collective-permute-start(f32[64,128]{1,0:T(8,128)S(1)} %get-tuple-element.43), channel_id=1, source_target_pairs={{2,1},{5,6},{10,9},{13,14},{17,18},{22,21},{25,26},{30,29},{34,33}... | collective-permute-start | bytes 98312 | tf_op jit(solution)/shard_map/ppermute | solution.py:346
  96.4 21.0 %collective-permute-start.13 = (f32[64,128]{1,0:T(8,128)S(1)}, f32[64,128]{1,0:T(8,128)S(1)}, u32[]{:S(2)}, u32[]{:S(2)}) collective-permute-start(f32[64,128]{1,0:T(8,128)S(1)} %get-tuple-element.44), channel_id=1, source_target_pairs={{2,0},{5,7},{10,8},{13,15},{17,19},{22,20},{25,27},{30,28},{34,32}... | collective-permute-start | bytes 98312 | tf_op jit(solution)/shard_map/ppermute | solution.py:346

commit v2 on v1

--- a/solution.py
+++ b/solution.py
@@ -51,6 +51,7 @@
         aug = jnp.concatenate([eye, m], axis=1)
         blocks.append([aug[8 * i : 8 * i + 8, :] for i in range(n)])
     sub = lax.broadcasted_iota(jnp.int32, wide, 0)
+    zero = jnp.minimum(jnp.abs(blocks[0][0]), 0.0)
     done = [[None] * n for _ in mats]
 
     def splat(v):
@@ -60,13 +61,14 @@
         jb, js = j // 8, j % 8
         for blk, out in zip(blocks, done):
             r0, r1, r2, r3 = [splat(blk[jb][js + a : js + a + 1, :]) for a in range(4)]
-
-            def at(row, b):
-                return splat(row[:, R + j + b : R + j + b + 1])
-
-            p00, p01, p02, p03 = [at(r0, b) for b in range(4)]
-            p11, p12, p13 = [at(r1, b) for b in range(1, 4)]
-            p22, p23, p33 = at(r2, 2), at(r2, 3), at(r3, 3)
+            near = [splat(blk[jb][:, R + j + t : R + j + t + 1]) + zero for t in range(4)]
+
+            def at(a, b):
+                return splat(near[b][js + a : js + a + 1, :])
+
+            p00, p01, p02, p03 = [at(0, b) for b in range(4)]
+            p11, p12, p13 = [at(1, b) for b in range(1, 4)]
+            p22, p23, p33 = at(2, 2), at(2, 3), at(3, 3)
             i1 = 1.0 / (p00 * p11 - p01 * p01)
             a00, a01, a11 = p11 * i1, -p01 * i1, p00 * i1
             t00, t01 = a00 * p02 + a01 * p12, a00 * p03 + a01 * p13
@@ -84,7 +86,7 @@
             for i in range(jb, n):
                 if i == jb and js == 4:
                     continue
-                c = [splat(blk[i][:, R + j + t : R + j + t + 1]) for t in range(4)]
+                c = near if i == jb else [splat(blk[i][:, R + j + t : R + j + t + 1]) for t in range(4)]
                 up = (c[0] * q0 + c[1] * q1) + (c[2] * q2 + c[3] * q3)
                 blk[i] = blk[i] - (jnp.where(sub >= 4, up, 0.0) if i == jb else up)
             if chol:
@@ -128,52 +130,85 @@
     return core, z, g, o, 2 * o - 3
 
 
-def interleave(core, own_ref, oth_ref, pan):
-    for c in range(16):
-        pan[:, c, pl.ds(core, 1), :, :] = own_ref[c][:, None]
-        pan[:, c, pl.ds(1 - core, 1), :, :] = oth_ref[c][:, None]
-
-
-def leaf_y(w_ref, tile_ref, own_ref, oth_ref, sk_ref, y_ref, inner_ref, pan):
+def half_rows(ref, k, c):
+    return ref[k, :, pl.ds(c, 1), :, :].reshape(512, 2 * R)
+
+
+def panel_rows(ref, k):
+    return ref[:, k, :, :].reshape(512, 2 * R)
+
+
+def core_major(sk):
+    lane = lax.broadcasted_iota(jnp.int32, (R, 128), 1)
+    halves = [[], []]
+    for m in range(4):
+        a, b = sk[:, 256 * m : 256 * m + 128], sk[:, 256 * m + 128 : 256 * m + 256]
+        a64, a96 = pltpu.roll(a, 64, 1), pltpu.roll(a, 96, 1)
+        b32, b64 = pltpu.roll(b, 32, 1), pltpu.roll(b, 64, 1)
+        for half, parts in zip(halves, ((a, a96, b64, b32), (a96, a64, b32, b))):
+            low = jnp.where(lane < 32, parts[0], parts[1])
+            high = jnp.where(lane < 96, parts[2], parts[3])
+            half.append(jnp.where(lane < 64, low, high))
+    return jnp.concatenate(halves[0] + halves[1], axis=1)
+
+
+def leaf_pre(tile_ref, own_ref, sk_ref, part_ref, vt_ref, split_ref):
     core = place()[0]
-    interleave(core, own_ref, oth_ref, pan)
-    sh, sl = split(sk_ref[...])
+    sh, sl = split(core_major(sk_ref[...]))
+    split_ref[:R] = sh
+    split_ref[R:] = sl
     r = lax.broadcasted_iota(jnp.int32, (R, 2 * R), 0)
     c = lax.broadcasted_iota(jnp.int32, (R, 2 * R), 1)
     pick = jnp.where(c == r + R, 1.0, 0.0).astype(BF16)
+    so = split_ref[:, pl.ds(pl.multiple_of(core * 512, 512), 512)]
+    for k in range(8):
+        vt = mm(pick, half_rows(tile_ref, k, core), NT).astype(BF16)
+        vt_ref[k] = mm(pick, half_rows(tile_ref, k, 1 - core), NT).astype(BF16)
+        part_ref[k] = mm(jnp.concatenate([so, vt], axis=0), panel_rows(own_ref, k))
+
+
+def leaf_y(w_ref, tile_ref, oth_ref, part_ref, vt_ref, split_ref, y_ref, inner_ref):
+    core = place()[0]
+    so = split_ref[:, pl.ds(pl.multiple_of((1 - core) * 512, 512), 512)]
     zero = jnp.zeros((R, R), F32)
-    acc = jnp.zeros((R, 1024), F32)
-    for k in range(8):
-        tile = tile_ref[k]
-        pan_k = pan[k].reshape(1024, 2 * R)
-        vt = mm(pick, tile, NT).astype(BF16)
-        res = mm(jnp.concatenate([sh, sl, vt], axis=0), pan_k)
-        proj = (res[:R] + res[R : 2 * R])[:, :R]
-        inner = res[2 * R :][:, R:] * w_ref[k].astype(F32)
-        inner_ref[k] = inner
-        dt = jnp.concatenate([dot3(proj, inner, NT), zero], axis=1)
-        dh, dl = split(dt)
-        out = mm(jnp.concatenate([dh, dl], axis=0), tile, NT)
-        acc = acc + (out[:R] + out[R:])
+    acc = None
+    for p in range(4):
+        dts = []
+        for k in (2 * p, 2 * p + 1):
+            res = part_ref[k] + mm(jnp.concatenate([so, vt_ref[k]], axis=0), panel_rows(oth_ref, k))
+            proj = (res[:R] + res[R : 2 * R])[:, :R]
+            inner = res[2 * R :][:, R:] * w_ref[k].astype(F32)
+            inner_ref[k] = inner
+            dts += [dot3(proj, inner, NT), zero]
+        dh, dl = split(jnp.concatenate(dts, axis=1))
+        tiles = jnp.concatenate([tile_ref[k].reshape(1024, 2 * R) for k in (2 * p, 2 * p + 1)], axis=1)
+        out = mm(jnp.concatenate([dh, dl], axis=0), tiles, NT)
+        out = out[:R] + out[R:]
+        acc = out if acc is None else acc + out
     y_ref[...] = acc
 
 
-def leaf_x(tile_ref, own_ref, oth_ref, y_ref, inner_ref, x_ref, pan):
+def leaf_x(tile_ref, own_ref, oth_ref, y_ref, inner_ref, x_ref):
     core = place()[0]
-    interleave(core, own_ref, oth_ref, pan)
     yh, yl = split(y_ref[...])
     ys = jnp.concatenate([yh, yl], axis=0)
     zero = jnp.zeros((R, R), F32)
-    acc = jnp.zeros((R, 1024), F32)
-    for k in range(8):
-        pan_k = pan[k].reshape(1024, 2 * R)
-        ht = mm(ys, tile_ref[k])
-        ht = (ht[:R] + ht[R:])[:, :R]
-        et = jnp.concatenate([dot3(ht, inner_ref[k]), zero], axis=1)
-        eh, el = split(et)
-        out = mm(jnp.concatenate([eh, el], axis=0), pan_k, NT)
-        acc = acc + (out[:R] + out[R:])
-    x_ref[...] = acc
+    accs = [None, None]
+    for p in range(4):
+        ks = (2 * p, 2 * p + 1)
+        ht = mm(ys, jnp.concatenate([tile_ref[k].reshape(1024, 2 * R) for k in ks], axis=1))
+        ht = ht[:R] + ht[R:]
+        ets = []
+        for i, k in enumerate(ks):
+            ets += [dot3(ht[:, 2 * R * i : 2 * R * i + R], inner_ref[k]), zero]
+        eh, el = split(jnp.concatenate(ets, axis=1))
+        es = jnp.concatenate([eh, el], axis=0)
+        for h, ref in enumerate((own_ref, oth_ref)):
+            out = mm(es, jnp.concatenate([panel_rows(ref, k) for k in ks], axis=1), NT)
+            out = out[:R] + out[R:]
+            accs[h] = out if accs[h] is None else accs[h] + out
+    x_ref[:, pl.ds(pl.multiple_of(core * 512, 512), 512)] = accs[0]
+    x_ref[:, pl.ds(pl.multiple_of((1 - core) * 512, 512), 512)] = accs[1]
 
 
 def lanes(mats):
@@ -237,10 +272,9 @@
     g = place()[2]
     sib = g + 1 - 2 * (g % 2)
     for dst, blocks in ((send_ref, (sib, 3 - sib)), (keep_ref, (g, 3 - g))):
-        for i, block in enumerate(blocks):
-            at = pl.multiple_of(block * 256, 256)
-            xh, xl = split(rows_of([x[:, pl.ds(at, 256)] for x in refs]))
-            dst[:, 256 * i : 256 * i + 256] = mm(qh, xh) + (mm(qh, xl) + mm(ql, xh))
+        spots = [pl.ds(pl.multiple_of(512 * c + block * 128, 128), 128) for block in blocks for c in range(2)]
+        xh, xl = split(rows_of([lanes([x[:, at] for at in spots]) for x in refs]))
+        dst[...] = mm(qh, xh) + (mm(qh, xl) + mm(ql, xh))
 
 
 def merge_y(y0, y1, out_ref, k_ref, j_ref, s_ref):
@@ -290,7 +324,10 @@
 
 def root_out(w_ref, f_ref, x0, x1, o0, o1, o2, o3, buf):
     zt = dot3(f_ref[...], rows_of([x0[...], x1[...]])) * (1.0 / 32.0)
-    buf[...] = rows_of([w_ref[...], zt]).T
+    both = rows_of([w_ref[...], zt]).T
+    natural = rows_of([both[128 * c + 32 * j : 128 * c + 32 * j + 32] for j in range(4) for c in range(2)])
+    lane = lax.broadcasted_iota(jnp.int32, (256, 2 * R), 1)
+    buf[...] = jnp.where(lane < R, both, natural)
     _, z, g, o, e = place()
     mine = jnp.where(z == 4 * g + o, 1, 0)
 
@@ -368,14 +405,15 @@
 
 
 def local_update(tiles, own, oth, nonnull, sketch, rows, upd):
-    pan = pltpu.VMEM((8, 16, 2, 32, 128), BF16)
-    tiles = tiles.reshape(8, 1024, 2 * R)
+    tiles = tiles.reshape(8, 16, 2, 32, 2 * R)
+    pre = (shape(8, 3 * R, 2 * R), shape(8, R, 512, dtype=BF16), shape(2 * R, 1024, dtype=BF16))
+    part, vt, halves = call(leaf_pre, pre, 0, [tiles, own, sketch])
     y, inner = call(
-        leaf_y, (shape(R, 1024), shape(8, R, R)), 1, [nonnull, tiles, own, oth, sketch], scratch=[pan]
+        leaf_y, (shape(R, 1024), shape(8, R, R)), 1, [nonnull, tiles, oth, part, vt, halves]
     )
 
     def leaf_x_of(y):
-        return call(leaf_x, shape(R, 1024), 0, [tiles, own, oth, y, inner], scratch=[pan])
+        return call(leaf_x, shape(R, 1024), 0, [tiles, own, oth, y, inner])
 
     return tree(y, leaf_x_of, rows, upd)
 

time: 120 us -> 116 us (0.967)
  the two profiles are of different devices: /device:TPU:1 before, /device:TPU:8 now
where the time goes in v2:
time: 116 us; the launch traced here: 115 us
  waiting for transfers between devices  33.3 us (29%)
  Pallas kernels  29.1 us (25%)
  starting transfers between devices  27.8 us (24%)
  blocking collectives  22.9 us (20%)
  local copies, waits for them, and re-layouts  1.19 us (1%)
    ppermute x13, waiting for transfers between devices, send(): return lax.ppermute(v, ('rows', 'upd'), perm)  32.2 us
    pallas_call x9, Pallas kernels, call(): return kernel(*args)  29.1 us
    ppermute x13, starting transfers between devices, send(): return lax.ppermute(v, ('rows', 'upd'), perm)  25.8 us
    all_to_all x1, blocking collectives, body(): own = lax.all_to_all(blocks, 'rows', 0, 0, axis_index_groups=same)  22.9 us
  transfers between devices with their start and end apart: 14, of which 3 were waited for; matrix products, arithmetic and copies ran while one was open for 0% of the time, Pallas kernels for 14%

profile of v2, /device:TPU:8, one launch (start us, length us, event | category | flops | bytes accessed | tf_op | source)
XLA Modules:
  0.0 115.2 jit_solution(13459962128268845946)
XLA Ops:
  0.0 0.0 copy-start.1
  0.0 0.0 copy-start
  0.0 1.2 %broadcast_in_dim.4 = bf16[16,8,32,128]{3,2,1,0:T(8,128)(2,1)S(1)} broadcast(bf16[8,32,128]{2,1,0:T(8,128)(2,1)} %param.5), dimensions={1,2,3} | broadcast | bytes 1114112 | tf_op jit(solution)/shard_map/broadcast_in_dim | solution.py:424
  1.2 22.9 %all_to_all.5.own_ref = bf16[16,8,32,128]{3,2,1,0:T(8,128)(2,1)S(1)} all-to-all(bf16[16,8,32,128]{3,2,1,0:T(8,128)(2,1)S(1)} %broadcast_in_dim.4), channel_id=1, replica_groups={{0,32,64,96,128,160,192,224,256,288,320,352,384,416,448,480},{16,48,80,..., dimensions={0} | all-to-all | bytes 2097152 | tf_op jit(solution)/shard_map/all_to_all | solution.py:425
  24.1 0.0 copy-start.2
  24.1 2.0 %collective-permute-start = (bf16[16,8,32,128]{3,2,1,0:T(8,128)(2,1)S(1)}, bf16[16,8,32,128]{3,2,1,0:T(8,128)(2,1)S(1)}, u32[]{:S(2)}, u32[]{:S(2)}) collective-permute-start(bf16[16,8,32,128]{3,2,1,0:T(8,128)(2,1)S(1)} %all_to_all.5.own_ref), channel_id=1, source_target_pairs={{0,16},{16,0},{32,48},{48,32},{64,80},{80,64},{96,112},{112,96},{1... | collective-permute-start | bytes 3145736 | tf_op jit(solution)/shard_map/ppermute | solution.py:426
  26.2 0.0 copy-done.1
  26.2 0.0 copy-done
  26.2 1.5 %shard_map.46 = (f32[8,192,128]{2,1,0:T(8,128)S(1)}, bf16[8,64,512]{2,1,0:T(8,128)(2,1)S(1)}, bf16[128,1024]{1,0:T(8,128)(2,1)S(1)}) custom-call(bf16[8,16,2,32,128]{4,3,2,1,0:T(8,128)(2,1)S(1)} %bitcast.4, bf16[16,8,32,128]{3,2,1,0:T(8,128)(2,1)S(1)} %all_to_all.5.own_ref, f32[64,1024]{1,0:T(8,128)S(1)} %copy-done.1), custom_call_target="tpu_custom_call" | custom-call | flops 100000000 | bytes 1000000 | tf_op jit(solution)/shard_map/pallas_call | solution.py:357
  27.7 1.1 collective-permute-done.oth_ref
  28.8 0.0 copy-done.2
  28.8 4.0 %shard_map.47 = (f32[64,1024]{1,0:T(8,128)S(1)}, f32[8,64,64]{2,1,0:T(8,128)S(1)}) custom-call(s32[8]{0:T(128)S(1)} %bitcast.7, bf16[8,16,2,32,128]{4,3,2,1,0:T(8,128)(2,1)S(1)} %bitcast.5, bf16[16,8,32,128]{3,2,1,0:T(8,128)(2,1)S(1)} %collective-permute-done.oth_ref, f32[8,192,128]{2,1,0:T(8,128)S(1)} %get-tuple-element.28.part_ref, ...), custom_call_target="tpu_custom_call" | custom-call | flops 100000000 | bytes 1000000 | tf_op jit(solution)/shard_map/pallas_call | solution.py:357
  32.8 4.8 %collective-permute-start.3 = (f32[64,1024]{1,0:T(8,128)S(1)}, f32[64,1024]{1,0:T(8,128)S(1)}, u32[]{:S(2)}, u32[]{:S(2)}) collective-permute-start(f32[64,1024]{1,0:T(8,128)S(1)} %get-tuple-element.31.y0.y_ref), channel_id=1, source_target_pairs={{0,2},{7,5},{8,10},{15,13},{19,17},{20,22},{27,25},{28,30},{32,34}... | collective-permute-start | bytes 786440 | tf_op jit(solution)/shard_map/ppermute | solution.py:383
  37.6 0.7 collective-permute-start.2
  38.3 0.7 collective-permute-start.1
  39.0 4.9 %collective-permute-done.3.y3 = f32[64,1024]{1,0:T(8,128)S(1)} collective-permute-done((f32[64,1024]{1,0:T(8,128)S(1)}, f32[64,1024]{1,0:T(8,128)S(1)}, u32[]{:S(2)}, u32[]{:S(2)}) %collective-permute-start.3) | collective-permute-done | bytes 262176 | tf_op jit(solution)/shard_map/ppermute | solution.py:383
  43.9 0.0 collective-permute-done.2.y2
  43.9 0.0 collective-permute-done.1.y1
  43.9 8.3 %shard_map.48 = (f32[64,1024]{1,0:T(8,128)S(1)}, f32[256,256]{1,0:T(8,128)S(1)}, f32[6,64,64]{2,1,0:T(8,128)S(1)}, f32[6,8,128]{2,1,0:T(8,128)S(1)}) custom-call(f32[64,1024]{1,0:T(8,128)S(1)} %get-tuple-element.31.y0.y_ref, f32[64,1024]{1,0:T(8,128)S(1)} %collective-permute-done.1.y1, f32[64,1024]{1,0:T(8,128)S(1)} %collective-permute-done.2.y2, ...), custom_call_target="tpu_custom_call" | custom-call | flops 100000000 | bytes 1000000 | tf_op jit(solution)/shard_map/pallas_call | solution.py:357
  52.2 0.7 collective-permute-start.4
  52.9 2.2 %shard_map.51.x0 = f32[64,1024]{1,0:T(8,128)S(1)} custom-call(bf16[8,16,2,32,128]{4,3,2,1,0:T(8,128)(2,1)S(1)} %bitcast.6, bf16[16,8,32,128]{3,2,1,0:T(8,128)(2,1)S(1)} %all_to_all.5.own_ref, bf16[16,8,32,128]{3,2,1,0:T(8,128)(2,1)S(1)} %collective-permute-done.oth_ref, f32[64,1024]{1,0:T(8,128)S(1)} %get-tuple-element.31.y0.y_ref, ...), custom_call_target="tpu_custom_call" | custom-call | flops 100000000 | bytes 1000000 | tf_op jit(solution)/shard_map/pallas_call | solution.py:357
  55.0 12.8 %collective-permute-start.8 = (f32[64,1024]{1,0:T(8,128)S(1)}, f32[64,1024]{1,0:T(8,128)S(1)}, u32[]{:S(2)}, u32[]{:S(2)}) collective-permute-start(f32[64,1024]{1,0:T(8,128)S(1)} %shard_map.51.x0), channel_id=1, source_target_pairs={{0,2},{7,5},{8,10},{15,13},{19,17},{20,22},{27,25},{28,30},{32,34}... | collective-permute-start | bytes 786440 | tf_op jit(solution)/shard_map/ppermute | solution.py:383
  67.8 0.7 collective-permute-start.7
  68.5 0.9 collective-permute-start.6
  69.4 0.0 collective-permute-done.4.y1
  69.4 3.9 %shard_map.49 = (f32[64,1024]{1,0:T(8,128)S(1)}, f32[128,128]{1,0:T(8,128)S(1)}, f32[2,64,64]{2,1,0:T(8,128)S(1)}, f32[2,8,128]{2,1,0:T(8,128)S(1)}) custom-call(f32[64,1024]{1,0:T(8,128)S(1)} %get-tuple-element.32.y0, f32[64,1024]{1,0:T(8,128)S(1)} %collective-permute-done.4.y1), custom_call_target="tpu_custom_call" | custom-call | flops 100000000 | bytes 1000000 | tf_op jit(solution)/shard_map/pallas_call | solution.py:357
  73.3 0.7 collective-permute-start.5
  74.0 0.0 collective-permute-done.8.x3
  74.0 0.0 collective-permute-done.7.x2
  74.0 0.0 collective-permute-done.6.x1
  74.0 1.8 %shard_map.52 = (f32[64,512]{1,0:T(8,128)S(1)}, f32[64,512]{1,0:T(8,128)S(1)}) custom-call(f32[64,1024]{1,0:T(8,128)S(1)} %shard_map.51.x0, f32[64,1024]{1,0:T(8,128)S(1)} %collective-permute-done.6.x1, f32[64,1024]{1,0:T(8,128)S(1)} %collective-permute-done.7.x2, f32[64,1024]{1,0:T(8,128)S(1)} %collective-permute-done.8.x3, ...), custom_call_target="tpu_custom_call" | custom-call | flops 100000000 | bytes 1000000 | tf_op jit(solution)/shard_map/pallas_call | solution.py:357
  75.8 0.7 collective-permute-start.9
  76.5 0.0 collective-permute-done.9.x1
  76.5 0.7 shard_map.53
  77.2 0.7 collective-permute-start.10
  77.8 0.0 collective-permute-done.5.y1
  77.9 6.5 %shard_map.50 = (f32[64,256]{1,0:T(8,128)S(1)}, f32[64,128]{1,0:T(8,128)S(1)}) custom-call(f32[64,1024]{1,0:T(8,128)S(1)} %get-tuple-element.33.y0, f32[64,1024]{1,0:T(8,128)S(1)} %collective-permute-done.5.y1), custom_call_target="tpu_custom_call" | custom-call | flops 100000000 | bytes 1000000 | tf_op jit(solution)/shard_map/pallas_call | solution.py:357
  84.3 0.0 collective-permute-done.10.x1
  84.3 0.3 shard_map.54
  84.6 0.7 collective-permute-start.11
  85.3 0.7 collective-permute-start.12
  86.0 1.3 %collective-permute-start.13 = (f32[64,128]{1,0:T(8,128)S(1)}, f32[64,128]{1,0:T(8,128)S(1)}, u32[]{:S(2)}, u32[]{:S(2)}) collective-permute-start(f32[64,128]{1,0:T(8,128)S(1)} %get-tuple-element.50), channel_id=1, source_target_pairs={{2,0},{5,7},{10,8},{13,15},{17,19},{22,20},{25,27},{30,28},{34,32}... | collective-permute-start | bytes 98312 | tf_op jit(solution)/shard_map/ppermute | solution.py:383
  87.3 0.0 collective-permute-done.11
  87.3 0.0 collective-permute-done.12
  87.3 27.3 %collective-permute-done.13 = f32[64,128]{1,0:T(8,128)S(1)} collective-permute-done((f32[64,128]{1,0:T(8,128)S(1)}, f32[64,128]{1,0:T(8,128)S(1)}, u32[]{:S(2)}, u32[]{:S(2)}) %collective-permute-start.13) | collective-permute-done | bytes 32800 | tf_op jit(solution)/shard_map/ppermute | solution.py:383
  114.6 0.6 add_bitcast_fusion
Async XLA Ops:
  0.0 26.2 %copy-start.1 = (f32[64,1024]{1,0:T(8,128)S(1)}, f32[64,1024]{1,0:T(8,128)}, u32[]{:S(2)}) copy-start(f32[64,1024]{1,0:T(8,128)} %sk_ref.1) | copy-start | bytes 786436
  0.0 26.2 %copy-start = (bf16[1,8,1024,128]{3,2,1,0:T(8,128)(2,1)S(1)}, bf16[1,8,1024,128]{3,2,1,0:T(8,128)(2,1)}, u32[]{:S(2)}) copy-start(bf16[1,8,1024,128]{3,2,1,0:T(8,128)(2,1)} %param.4) | copy-start | bytes 6291460
  24.1 4.7 %copy-start.2 = (s32[1,8]{1,0:T(1,128)S(1)}, s32[1,8]{1,0:T(1,128)}, u32[]{:S(2)}) copy-start(s32[1,8]{1,0:T(1,128)} %param.6) | copy-start | bytes 100
  24.1 4.7 %collective-permute-start = (bf16[16,8,32,128]{3,2,1,0:T(8,128)(2,1)S(1)}, bf16[16,8,32,128]{3,2,1,0:T(8,128)(2,1)S(1)}, u32[]{:S(2)}, u32[]{:S(2)}) collective-permute-start(bf16[16,8,32,128]{3,2,1,0:T(8,128)(2,1)S(1)} %all_to_all.5.own_ref), channel_id=1, source_target_pairs={{0,16},{16,0},{32,48},{48,32},{64,80},{80,64},{96,112},{112,96},{1... | collective-permute-start | bytes 3145736 | tf_op jit(solution)/shard_map/ppermute | solution.py:426
  32.8 11.1 %collective-permute-start.3 = (f32[64,1024]{1,0:T(8,128)S(1)}, f32[64,1024]{1,0:T(8,128)S(1)}, u32[]{:S(2)}, u32[]{:S(2)}) collective-permute-start(f32[64,1024]{1,0:T(8,128)S(1)} %get-tuple-element.31.y0.y_ref), channel_id=1, source_target_pairs={{0,2},{7,5},{8,10},{15,13},{19,17},{20,22},{27,25},{28,30},{32,34}... | collective-permute-start | bytes 786440 | tf_op jit(solution)/shard_map/ppermute | solution.py:383
  37.6 6.3 %collective-permute-start.2 = (f32[64,1024]{1,0:T(8,128)S(1)}, f32[64,1024]{1,0:T(8,128)S(1)}, u32[]{:S(2)}, u32[]{:S(2)}) collective-permute-start(f32[64,1024]{1,0:T(8,128)S(1)} %get-tuple-element.31.y0.y_ref), channel_id=1, source_target_pairs={{1,2},{6,5},{9,10},{14,13},{18,17},{21,22},{26,25},{29,30},{33,34}... | collective-permute-start | bytes 786440 | tf_op jit(solution)/shard_map/ppermute | solution.py:383
  38.3 5.6 %collective-permute-start.1 = (f32[64,1024]{1,0:T(8,128)S(1)}, f32[64,1024]{1,0:T(8,128)S(1)}, u32[]{:S(2)}, u32[]{:S(2)}) collective-permute-start(f32[64,1024]{1,0:T(8,128)S(1)} %get-tuple-element.31.y0.y_ref), channel_id=1, source_target_pairs={{3,2},{4,5},{11,10},{12,13},{16,17},{23,22},{24,25},{31,30},{35,34... | collective-permute-start | bytes 786440 | tf_op jit(solution)/shard_map/ppermute | solution.py:383
  52.2 17.2 %collective-permute-start.4 = (f32[64,1024]{1,0:T(8,128)S(1)}, f32[64,1024]{1,0:T(8,128)S(1)}, u32[]{:S(2)}, u32[]{:S(2)}) collective-permute-start(f32[64,1024]{1,0:T(8,128)S(1)} %get-tuple-element.32.y0), channel_id=1, source_target_pairs={{2,5},{5,2},{10,13},{13,10},{17,22},{22,17},{25,30},{30,25},{34,37... | collective-permute-start | bytes 786440 | tf_op jit(solution)/shard_map/ppermute | solution.py:383
  55.0 18.9 %collective-permute-start.8 = (f32[64,1024]{1,0:T(8,128)S(1)}, f32[64,1024]{1,0:T(8,128)S(1)}, u32[]{:S(2)}, u32[]{:S(2)}) collective-permute-start(f32[64,1024]{1,0:T(8,128)S(1)} %shard_map.51.x0), channel_id=1, source_target_pairs={{0,2},{7,5},{8,10},{15,13},{19,17},{20,22},{27,25},{28,30},{32,34}... | collective-permute-start | bytes 786440 | tf_op jit(solution)/shard_map/ppermute | solution.py:383
  67.8 6.1 %collective-permute-start.7 = (f32[64,1024]{1,0:T(8,128)S(1)}, f32[64,1024]{1,0:T(8,128)S(1)}, u32[]{:S(2)}, u32[]{:S(2)}) collective-permute-start(f32[64,1024]{1,0:T(8,128)S(1)} %shard_map.51.x0), channel_id=1, source_target_pairs={{1,2},{6,5},{9,10},{14,13},{18,17},{21,22},{26,25},{29,30},{33,34}... | collective-permute-start | bytes 786440 | tf_op jit(solution)/shard_map/ppermute | solution.py:383
  68.5 5.5 %collective-permute-start.6 = (f32[64,1024]{1,0:T(8,128)S(1)}, f32[64,1024]{1,0:T(8,128)S(1)}, u32[]{:S(2)}, u32[]{:S(2)}) collective-permute-start(f32[64,1024]{1,0:T(8,128)S(1)} %shard_map.51.x0), channel_id=1, source_target_pairs={{3,2},{4,5},{11,10},{12,13},{16,17},{23,22},{24,25},{31,30},{35,34... | collective-permute-start | bytes 786440 | tf_op jit(solution)/shard_map/ppermute | solution.py:383
  73.3 4.6 %collective-permute-start.5 = (f32[64,1024]{1,0:T(8,128)S(1)}, f32[64,1024]{1,0:T(8,128)S(1)}, u32[]{:S(2)}, u32[]{:S(2)}) collective-permute-start(f32[64,1024]{1,0:T(8,128)S(1)} %get-tuple-element.33.y0), channel_id=1, source_target_pairs={{2,13},{5,10},{10,5},{13,2},{17,30},{22,25},{25,22},{30,17},{34,45... | collective-permute-start | bytes 786440 | tf_op jit(solution)/shard_map/ppermute | solution.py:383
  75.8 0.7 collective-permute-start.9
  77.2 7.2 %collective-permute-start.10 = (f32[64,256]{1,0:T(8,128)S(1)}, f32[64,256]{1,0:T(8,128)S(1)}, u32[]{:S(2)}, u32[]{:S(2)}) collective-permute-start(f32[64,256]{1,0:T(8,128)S(1)} %get-tuple-element.46), channel_id=1, source_target_pairs={{2,13},{5,10},{10,5},{13,2},{17,30},{22,25},{25,22},{30,17},{34,45... | collective-permute-start | bytes 196616 | tf_op jit(solution)/shard_map/ppermute | solution.py:383
  84.6 2.6 %collective-permute-start.11 = (f32[64,128]{1,0:T(8,128)S(1)}, f32[64,128]{1,0:T(8,128)S(1)}, u32[]{:S(2)}, u32[]{:S(2)}) collective-permute-start(f32[64,128]{1,0:T(8,128)S(1)} %get-tuple-element.48), channel_id=1, source_target_pairs={{2,3},{5,4},{10,11},{13,12},{17,16},{22,23},{25,24},{30,31},{34,35... | collective-permute-start | bytes 98312 | tf_op jit(solution)/shard_map/ppermute | solution.py:383
  85.3 2.0 %collective-permute-start.12 = (f32[64,128]{1,0:T(8,128)S(1)}, f32[64,128]{1,0:T(8,128)S(1)}, u32[]{:S(2)}, u32[]{:S(2)}) collective-permute-start(f32[64,128]{1,0:T(8,128)S(1)} %get-tuple-element.49), channel_id=1, source_target_pairs={{2,1},{5,6},{10,9},{13,14},{17,18},{22,21},{25,26},{30,29},{34,33}... | collective-permute-start | bytes 98312 | tf_op jit(solution)/shard_map/ppermute | solution.py:383
  86.0 28.6 %collective-permute-start.13 = (f32[64,128]{1,0:T(8,128)S(1)}, f32[64,128]{1,0:T(8,128)S(1)}, u32[]{:S(2)}, u32[]{:S(2)}) collective-permute-start(f32[64,128]{1,0:T(8,128)S(1)} %get-tuple-element.50), channel_id=1, source_target_pairs={{2,0},{5,7},{10,8},{13,15},{17,19},{22,20},{25,27},{30,28},{34,32}... | collective-permute-start | bytes 98312 | tf_op jit(solution)/shard_map/ppermute | solution.py:383
